TPU v7x, 128 devices: a whole 4x4x4 slice. The times are simulated.
128 devices in a mesh: row: 32 (over z, y, core), col: 4 (over x).
Axes of the slice: x: 4, y: 4, z: 4, core: 2. Of those that a mesh axis runs over, the one named last changes fastest.
Arguments:
- tokens: bfloat16 [16384, 2048], P('row', 'col'), may hold values from -6 to 6
- cotangent: bfloat16 [16384, 2048], P('row', 'col'), may hold values from -6 to 6
- destination: int32 [16384], P('row'), may hold values from 0 to 16383, as said below
- segment_ids: int32 [16384], P('row'), may hold values from 0 to 7, as said below
- attn_gain: float32 [2048], replicated, may hold values from 0.5 to 1.5
- w_query: bfloat16 [2048, 2048], P('row', 'col'), may hold values from -0.125 to 0.125
- w_key: bfloat16 [2048, 256], P('row', 'col'), may hold values from -0.125 to 0.125
- w_value: bfloat16 [2048, 256], P('row', 'col'), may hold values from -0.125 to 0.125
- w_output: bfloat16 [2048, 2048], P('row', 'col'), may hold values from -0.5 to 0.5
- ffn_gain: float32 [2048], replicated, may hold values from 0.5 to 1.5
- w_gate: bfloat16 [2048, 5632], P('row', 'col'), may hold values from -0.125 to 0.125
- w_up: bfloat16 [2048, 5632], P('row', 'col'), may hold values from -0.125 to 0.125
- w_down: bfloat16 [2048, 5632], P('row', 'col'), may hold values from -0.078125 to 0.078125
Outputs:
- output: bfloat16 [16384, 2048], P('row', 'col')
- input_grad: bfloat16 [16384, 2048], P('row', 'col')
- attn_gain_grad: float32 [2048], P('row')
- w_query_grad: float32 [2048, 2048], P('row', 'col')
- w_key_grad: float32 [2048, 256], P('row', 'col')
- w_value_grad: float32 [2048, 256], P('row', 'col')
- w_output_grad: float32 [2048, 2048], P('row', 'col')
- ffn_gain_grad: float32 [2048], P('row')
- w_gate_grad: float32 [2048, 5632], P('row', 'col')
- w_up_grad: float32 [2048, 5632], P('row', 'col')
- w_down_grad: float32 [2048, 5632], P('row', 'col')
Inputs may be any that keep to these rules, and one draw needn't show every extreme that they name: `destination`: A permutation; the tokens of each aligned block of 512 arriving tokens go to exactly 16 places in each aligned block of 512 balanced places. `segment_ids`: within each aligned block of 512 places the ids start at 0 and rise by one where a new sequence begins, so a block holds at most 8 sequences; in every draw some block holds a single sequence of 512 tokens and some block holds 8 sequences.
All inputs are finite; a program needn't handle non-finite values.
Results may differ from a plain program's by a relative error of at most 0.028.
Values may be sent and summed in bfloat16 or wider, within the bound.
No kernel may reach another device: no remote copies, remote signals or barrier semaphores. Data moves between devices by JAX's collectives and lax.ppermute only.
A program may use at most 128 MiB of HBM per device.

v0:
```python
from functools import partial
import jax
import jax.numpy as jnp
from jax import lax
from jax.sharding import PartitionSpec as P

HEADS = 32
KV = 4
HD = 64
EPS = 1e-05
ROPE_BASE = 10000.0


def rope_tables(positions):
    half_width = HD // 2
    freqs = ROPE_BASE ** (-(jnp.arange(half_width, dtype=jnp.float32) * 2.0 / HD))
    angles = positions.astype(jnp.float32)[:, None] * freqs[None, :]
    return (jnp.cos(angles)[:, None, :], jnp.sin(angles)[:, None, :])


def rotate(values, cosine, sine):
    half_width = values.shape[-1] // 2
    first = values[..., :half_width]
    second = values[..., half_width:]
    return jnp.concatenate(
        [first * cosine - second * sine, second * cosine + first * sine], axis=-1
    )


def rotate_back(grads, cosine, sine):
    half_width = grads.shape[-1] // 2
    first = grads[..., :half_width]
    second = grads[..., half_width:]
    return jnp.concatenate(
        [first * cosine + second * sine, second * cosine - first * sine], axis=-1
    )


def positions_of(segment_ids):
    index = jnp.arange(segment_ids.shape[0], dtype=jnp.int32)
    change = jnp.concatenate([jnp.ones((1,), dtype=jnp.bool_), segment_ids[1:] != segment_ids[:-1]])
    starts = jnp.where(change, index, jnp.zeros_like(index))
    return index - lax.cummax(starts, axis=0)


def allowed_pairs(segment_ids):
    index = jnp.arange(segment_ids.shape[0], dtype=jnp.int32)
    return (segment_ids[:, None] == segment_ids[None, :]) & (index[None, :] <= index[:, None])


def rms_scale(values):
    return lax.rsqrt(jnp.mean(values * values, axis=-1, keepdims=True) + EPS)


def norm_back(values, inv_root, gain, grads):
    normed = values * inv_root
    scaled = grads * gain
    result = inv_root * (scaled - normed * jnp.mean(scaled * normed, axis=-1, keepdims=True))
    return (result, jnp.sum(grads * normed, axis=0))


def matmul(left, right):
    return jnp.dot(left, right, preferred_element_type=jnp.float32)


def head_scores(query_head, key_head, allowed, scale_factor):
    scores = matmul(query_head, key_head.T) * scale_factor
    return jnp.where(allowed, scores, -1e30)


def head_forward(inputs, key_heads, value_heads, allowed, scale_factor):
    query_head, kv_slot = inputs
    scores = head_scores(query_head, key_heads[kv_slot], allowed, scale_factor)
    peak = jnp.max(scores, axis=-1, keepdims=True)
    expo = jnp.exp(scores - peak)
    total = jnp.sum(expo, axis=-1, keepdims=True)
    probs = expo / total
    mixed = matmul(probs.astype(jnp.bfloat16), value_heads[kv_slot])
    return (mixed, (peak + jnp.log(total))[:, 0])


def head_backward(inputs, key_heads, value_heads, allowed, scale_factor):
    query_head, kv_slot, grad_head, log_total = inputs
    key_head = key_heads[kv_slot]
    value_head = value_heads[kv_slot]
    scores = head_scores(query_head, key_head, allowed, scale_factor)
    probs = jnp.exp(scores - log_total[:, None])
    prob_grad = matmul(grad_head, value_head.T)
    value_grad = matmul(probs.astype(jnp.bfloat16).T, grad_head)
    inner = jnp.sum(probs * prob_grad, axis=-1, keepdims=True)
    score_grad = (probs * (prob_grad - inner)).astype(jnp.bfloat16)
    query_grad = matmul(score_grad, key_head) * scale_factor
    key_grad = matmul(score_grad.T, query_head) * scale_factor
    return (query_grad, key_grad, value_grad)


def gather_rows(parts):
    widths = [part.shape[1] for part in parts]
    packed = lax.all_gather(jnp.concatenate(parts, axis=1), "row", axis=0, tiled=True)
    pieces = []
    offset = 0
    for width in widths:
        pieces.append(packed[:, offset : offset + width])
        offset += width
    return pieces


def scatter_rows(parts):
    columns = [part.reshape(part.shape[0], -1).astype(jnp.bfloat16) for part in parts]
    widths = [column.shape[1] for column in columns]
    packed = lax.psum_scatter(
        jnp.concatenate(columns, axis=1), "row", scatter_dimension=0, tiled=True
    ).astype(jnp.float32)
    pieces = []
    offset = 0
    for part, width in zip(parts, widths):
        piece = packed[:, offset : offset + width]
        pieces.append(piece.reshape(-1) if part.ndim == 1 else piece)
        offset += width
    return pieces


def body(
    tokens,
    cotangent,
    destination,
    segment_ids,
    attn_gain,
    w_query,
    w_key,
    w_value,
    w_output,
    ffn_gain,
    w_gate,
    w_up,
    w_down,
):
    row_count = tokens.shape[0]
    quarter = tokens.shape[1]
    col_start = lax.axis_index("col") * quarter
    group_size = HEADS // KV
    send_order = jnp.argsort(destination)
    slot_ids = destination[send_order] % row_count
    arrived_rows, arrived_grads, arrived_slots = (
        lax.all_to_all(tokens[send_order], "row", split_axis=0, concat_axis=0, tiled=True),
        lax.all_to_all(cotangent[send_order], "row", split_axis=0, concat_axis=0, tiled=True),
        lax.all_to_all(slot_ids, "row", split_axis=0, concat_axis=0, tiled=True),
    )
    placing = jnp.argsort(arrived_slots)
    full_rows, full_grads = (
        lax.all_gather(arrived_rows[placing], "col", axis=1, tiled=True),
        lax.all_gather(arrived_grads[placing], "col", axis=1, tiled=True),
    )
    query_w, key_w, value_w, output_w = gather_rows([w_query, w_key, w_value, w_output])
    cosine, sine = rope_tables(positions_of(segment_ids))
    allowed = allowed_pairs(segment_ids)
    rows_wide = full_rows.astype(jnp.float32)
    inv_one = rms_scale(rows_wide)
    normed_one = (rows_wide * inv_one * attn_gain).astype(jnp.bfloat16)
    query = matmul(normed_one, query_w)
    key_raw = matmul(normed_one, key_w)
    value_raw = matmul(normed_one, value_w)
    query_heads_count = query.shape[1] // HD
    kv_count = key_raw.shape[1] // HD
    query_rot = (
        rotate(query.reshape(row_count, query_heads_count, HD), cosine, sine)
        .astype(jnp.bfloat16)
        .transpose(1, 0, 2)
    )
    key_rot = (
        rotate(key_raw.reshape(row_count, kv_count, HD), cosine, sine)
        .astype(jnp.bfloat16)
        .transpose(1, 0, 2)
    )
    value_heads = value_raw.astype(jnp.bfloat16).reshape(row_count, kv_count, HD).transpose(1, 0, 2)
    kv_slots = jnp.arange(query_heads_count, dtype=jnp.int32) // group_size
    scale_factor = HD ** (-0.5)
    mixed_heads, log_totals = lax.map(
        partial(
            head_forward,
            key_heads=key_rot,
            value_heads=value_heads,
            allowed=allowed,
            scale_factor=scale_factor,
        ),
        (query_rot, kv_slots),
    )
    mixed = (
        mixed_heads.transpose(1, 0, 2)
        .reshape(row_count, query_heads_count * HD)
        .astype(jnp.bfloat16)
    )
    attn_terms = matmul(mixed, output_w.T)
    attn_full = lax.psum(attn_terms, "col")
    resid = rows_wide + attn_full
    inv_two = rms_scale(resid)
    normed_two = (resid * inv_two * ffn_gain).astype(jnp.bfloat16)
    resid_part = lax.dynamic_slice_in_dim(resid, col_start, quarter, 1)
    gate_w, up_w, down_w = gather_rows([w_gate, w_up, w_down])
    gate = matmul(normed_two, gate_w)
    upper = matmul(normed_two, up_w)
    sigmoid_gate = jax.nn.sigmoid(gate)
    activ = (gate * sigmoid_gate * upper).astype(jnp.bfloat16)
    ffn_share = lax.psum_scatter(
        matmul(activ, down_w.T).astype(jnp.bfloat16), "col", scatter_dimension=1, tiled=True
    ).astype(jnp.float32)
    output_share = (resid_part + ffn_share).astype(jnp.bfloat16)
    down_weight_grad = matmul(full_grads.T, activ)
    act_grad = matmul(full_grads, down_w)
    gate_grad = (act_grad * upper * sigmoid_gate * (1.0 + gate * (1.0 - sigmoid_gate))).astype(
        jnp.bfloat16
    )
    up_grad = (act_grad * gate * sigmoid_gate).astype(jnp.bfloat16)
    gate_weight_grad = matmul(normed_two.T, gate_grad)
    up_weight_grad = matmul(normed_two.T, up_grad)
    normed_terms_two = matmul(gate_grad, gate_w.T) + matmul(up_grad, up_w.T)
    normed_grad_two = lax.psum(normed_terms_two, "col")
    resid_norm_grad, ffn_gain_grad = norm_back(resid, inv_two, ffn_gain, normed_grad_two)
    resid_grad = full_grads.astype(jnp.float32) + resid_norm_grad
    attn_grad_low = resid_grad.astype(jnp.bfloat16)
    output_weight_grad = matmul(attn_grad_low.T, mixed)
    mixed_grad = matmul(attn_grad_low, output_w).astype(jnp.bfloat16)
    mixed_grad_heads = mixed_grad.reshape(row_count, query_heads_count, HD).transpose(1, 0, 2)
    query_grads, key_grads, value_grads = lax.map(
        partial(
            head_backward,
            key_heads=key_rot,
            value_heads=value_heads,
            allowed=allowed,
            scale_factor=scale_factor,
        ),
        (query_rot, kv_slots, mixed_grad_heads, log_totals),
    )
    query_grad = (
        rotate_back(query_grads.transpose(1, 0, 2), cosine, sine)
        .reshape(row_count, query_heads_count * HD)
        .astype(jnp.bfloat16)
    )
    key_sum = key_grads.reshape(kv_count, group_size, row_count, HD).sum(axis=1).transpose(1, 0, 2)
    key_grad = (
        rotate_back(key_sum, cosine, sine).reshape(row_count, kv_count * HD).astype(jnp.bfloat16)
    )
    value_sum = (
        value_grads.reshape(kv_count, group_size, row_count, HD).sum(axis=1).transpose(1, 0, 2)
    )
    value_grad = value_sum.reshape(row_count, kv_count * HD).astype(jnp.bfloat16)
    query_weight_grad = matmul(normed_one.T, query_grad)
    key_weight_grad = matmul(normed_one.T, key_grad)
    value_weight_grad = matmul(normed_one.T, value_grad)
    normed_terms_one = (
        matmul(query_grad, query_w.T) + matmul(key_grad, key_w.T) + matmul(value_grad, value_w.T)
    )
    normed_grad_one = lax.psum(normed_terms_one.astype(jnp.bfloat16), "col").astype(jnp.float32)
    rows_norm_grad, attn_gain_grad = norm_back(rows_wide, inv_one, attn_gain, normed_grad_one)
    rows_grad = resid_grad + rows_norm_grad
    input_share = lax.dynamic_slice_in_dim(rows_grad, col_start, quarter, 1).astype(jnp.bfloat16)
    (
        query_result,
        key_result,
        value_result,
        output_result,
        gate_result,
        up_result,
        down_result,
        attn_gain_result,
        ffn_gain_result,
    ) = scatter_rows(
        [
            query_weight_grad,
            key_weight_grad,
            value_weight_grad,
            output_weight_grad,
            gate_weight_grad,
            up_weight_grad,
            down_weight_grad,
            attn_gain_grad,
            ffn_gain_grad,
        ]
    )
    back_rows, back_grads = (
        lax.all_to_all(output_share[arrived_slots], "row", split_axis=0, concat_axis=0, tiled=True),
        lax.all_to_all(input_share[arrived_slots], "row", split_axis=0, concat_axis=0, tiled=True),
    )
    restore = jnp.argsort(send_order)
    return (
        back_rows[restore],
        back_grads[restore],
        attn_gain_result,
        query_result,
        key_result,
        value_result,
        output_result,
        ffn_gain_result,
        gate_result,
        up_result,
        down_result,
    )


def solution(mesh):
    placed = (
        P("row", "col"),
        P("row", "col"),
        P("row"),
        P("row"),
        P(),
        P("row", "col"),
        P("row", "col"),
        P("row", "col"),
        P("row", "col"),
        P(),
        P("row", "col"),
        P("row", "col"),
        P("row", "col"),
    )
    return jax.shard_map(
        body,
        mesh=mesh,
        in_specs=placed,
        out_specs=(
            P("row", "col"),
            P("row", "col"),
            P("row"),
            P("row", "col"),
            P("row", "col"),
            P("row", "col"),
            P("row", "col"),
            P("row"),
            P("row", "col"),
            P("row", "col"),
            P("row", "col"),
        ),
        check_vma=False,
    )
```

profile of v0, /device:TPU:1, one launch (start us, length us, event | category | flops | bytes accessed | tf_op | source)
XLA Modules:
  0.0 914.6 jit_solution(13303859457156370730)
XLA Ops:
  7.2 4.5 sort.45
  12.3 3.6 gather_fusion.1
  16.6 9.6 %all-to-all-start.1 = ((s32[32,16,1]{1,2,0:T(1,128)}), s32[32,16,1]{1,2,0:T(1,128)S(1)}, u32[]{:S(2)}, u32[]{:S(2)}) async-start(s32[32,16,1]{1,2,0:T(1,128)} %bitcast.2), calls=%async_computation.1 | async-start | bytes 32768 | tf_op jit(solution)/shard_map/all_to_all | solution.py:147
  26.2 2.6 gather_fusion
  28.9 4.2 all-to-all-done.1
  33.1 4.2 all-to-all-start
  38.6 3.8 sort.46
  42.4 6.5 all-to-all-done
  48.9 2.6 gather_fusion.2
  53.7 26.4 %all-gather.11.cloned.1.call-done = bf16[512,2048]{1,0:T(8,128)(2,1)} async-done(((bf16[512,512]{1,0:T(8,128)(2,1)}), bf16[512,2048]{1,0:T(8,128)(2,1)}) %all-gather.11.cloned.1.call-update) | async-done | bytes 2097168 | tf_op jit(solution)/shard_map/all_gather | solution.py:151
  80.0 2.1 fusion.54
  82.1 48.2 %all-gather.7.cloned.1.call-done = bf16[2048,1152]{1,0:T(8,128)(2,1)} async-done(((bf16[64,1152]{1,0:T(8,128)(2,1)}), bf16[2048,1152]{1,0:T(8,128)(2,1)}) %all-gather.7.cloned.1.call-update) | async-done | bytes 4718608 | tf_op jit(solution)/shard_map/all_gather | solution.py:99
  130.3 3.6 fusion.67
  135.6 1.9 convolution_bitcast_fusion.2
  138.0 2.0 fusion.72
  140.1 25.1 %while.32 = (s32[]{:T(128)}, bf16[8,512,64]{1,2,0:T(8,128)(2,1)S(1)}, f32[8,512]{1,0:T(8,128)}, bf16[8,512,64]{2,1,0:T(8,128)(2,1)}, bf16[1,512,64]{2,1,0:T(8,12...) while((s32[]{:T(128)}, bf16[8,512,64]{1,2,0:T(8,128)(2,1)S(1)}, ...), condition=%wide.region_8.9_spmd.clone.clone, body=%wide.region_5.8_spmd.clone.sunk.clone | while | flops 69991936 | bytes 3694689 | solution.py:178
  166.0 5.0 fusion.63
  172.0 2.0 gather_fusion.5
  174.0 16.6 %all_to_all.60 = bf16[32,16,512]{2,1,0:T(8,128)(2,1)S(1)} all-to-all(bf16[32,16,512]{2,1,0:T(8,128)(2,1)S(1)} %bitcast.184), channel_id=1, replica_groups=mesh['row'=32,'col'=4] {'row'}, dimensions={0} | all-to-all | bytes 1048576 | tf_op jit(solution)/shard_map/all_to_all | solution.py:146
  190.6 2.6 gather_fusion.6
  195.2 67.6 %all-reduce.4.cloned.1.call-done = f32[512,2048]{1,0:T(8,128)} async-done(((f32[512,2048]{1,0:T(8,128)}), f32[512,2048]{1,0:T(8,128)}) %all-reduce.4.cloned.1.call-update) | async-done | bytes 4194320 | tf_op jit(solution)/shard_map/psum | solution.py:194
  262.7 2.8 multiply_reduce_fusion.4
  265.6 2.0 copy-done.2
  269.3 26.3 %all-gather.13.cloned.1.call-done = bf16[512,2048]{1,0:T(8,128)(2,1)} async-done(((bf16[512,512]{1,0:T(8,128)(2,1)}), bf16[512,2048]{1,0:T(8,128)(2,1)}) %all-gather.13.cloned.1.call-update) | async-done | bytes 2097168 | tf_op jit(solution)/shard_map/all_gather | solution.py:152
  295.7 76.7 %all-gather.9.cloned.1.call-done = bf16[2048,4224]{1,0:T(8,128)(2,1)} async-done(((bf16[64,4224]{1,0:T(8,128)(2,1)}), bf16[2048,4224]{1,0:T(8,128)(2,1)}) %all-gather.9.cloned.1.call-update) | async-done | bytes 17301520 | tf_op jit(solution)/shard_map/all_gather | solution.py:99
  372.4 6.5 fusion.41
  378.9 2.3 copy-done.31
  381.3 5.0 fusion.47
  386.2 7.3 multiply_convert_fusion.4
  393.6 5.4 fusion.45
  398.9 5.0 fusion.55
  404.0 9.7 %all-reduce.8.cloned.1.call-start = ((), (), s32[]{:S(2)}) async-start(), calls=%async_computation.12 | async-start | bytes 4194304 | tf_op jit(solution)/shard_map/psum | solution.py:253
  413.7 82.1 %all-reduce.6.cloned.1.call-done = f32[512,2048]{1,0:T(8,128)} async-done(((f32[512,2048]{1,0:T(8,128)}), f32[512,2048]{1,0:T(8,128)}) %all-reduce.6.cloned.1.call-update) | async-done | bytes 4194320 | tf_op jit(solution)/shard_map/psum | solution.py:217
  495.9 4.6 multiply_reduce_fusion.1
  501.8 2.7 multiply_add_fusion
  504.5 1.9 copy-done.7
  506.4 3.7 fusion.69
  511.6 50.9 %while.33 = (s32[]{:T(128)}, f32[8,512,64]{1,2,0:T(8,128)}, f32[8,512,64]{1,2,0:T(8,128)}, f32[8,512,64]{1,2,0:T(8,128)}, bf16[8,512,64]{2,1,0:T(8,128)(2,1)}, /...) while((s32[]{:T(128)}, f32[8,512,64]{1,2,0:T(8,128)}, ...), condition=%wide.region_17.18_spmd.clone.clone, body=%wide.region_15.17_spmd.clone.sunk.clone | while | flops 170982912 | bytes 9126013 | solution.py:224
  540.6 1.9 fusion.176
  567.5 2.9 fusion.65
  572.2 3.2 add_convert_fusion
  575.5 7.9 fusion.58
  583.5 7.9 convolution_convert_fusion.2
  591.4 5.3 convolution_convert_fusion.1
  596.7 5.0 convolution_convert_fusion
  603.4 2.7 convolution_convert_fusion.4
  606.1 2.6 convolution_convert_fusion.3
  608.7 25.4 %all-reduce.8.cloned.1.call-done = bf16[512,2048]{1,0:T(8,128)(2,1)} async-done(((bf16[512,2048]{1,0:T(8,128)(2,1)}), bf16[512,2048]{1,0:T(8,128)(2,1)}) %all-reduce.8.cloned.1.call-update) | async-done | bytes 2097168 | tf_op jit(solution)/shard_map/psum | solution.py:253
  634.1 6.1 fusion.53
  640.2 93.2 %concatenate.53 = bf16[2048,5378]{0,1:T(8,128)(2,1)} concatenate(bf16[2048,512]{0,1:T(8,128)(2,1)} %convolution_convert_fusion.4, bf16[2048,64]{0,1:T(8,128)(2,1)S(1)} %convolution_convert_fusion.6, bf16[2048,64]{0,1:T(8,128)(2,1)S(1)} %convolution_convert_fusion.5, bf16[2048,512]{0,1:T(8,128)(2,1)} %convolution_convert_fusion.3, bf16[2048,1408]{0,1:T(8,128)(2,1)} %convolution_convert_fusion.2, ...), dimensions={1} | concatenate | bytes 44056576 | tf_op jit(solution)/shard_map/concatenate | solution.py:112
  733.5 28.4 %copy.67 = bf16[2048,5378]{1,0:T(8,128)(2,1)} copy(bf16[2048,5378]{0,1:T(8,128)(2,1)} %concatenate.53) | data formatting | bytes 44056576
  764.3 2.6 gather_fusion.3
  766.9 7.7 all-to-all-start.2
  774.6 2.5 fusion.73
  777.1 2.6 gather_fusion.7
  779.8 6.4 all-to-all-done.2
  786.1 4.4 all-to-all-start.4
  790.5 3.8 sort.47
  794.3 2.6 gather_fusion.4
  796.9 5.1 all-to-all-done.4
  802.1 2.6 gather_fusion.8
  804.7 89.5 %reduce-scatter.7.cloned.1.call-done = bf16[64,5378]{1,0:T(8,128)(2,1)} async-done(((bf16[2048,5378]{1,0:T(8,128)(2,1)}), bf16[64,5378]{1,0:T(8,128)(2,1)}) %reduce-scatter.7.cloned.1.call-update) | async-done | bytes 688400
  894.2 2.0 copy.68
  903.6 2.1 copy.64
  (248 shorter events, 109.3 us)
Async XLA Ops:
  7.2 19.0 %copy-start = (bf16[512,512]{1,0:T(8,128)(2,1)S(1)}, bf16[512,512]{1,0:T(8,128)(2,1)}, u32[]{:S(2)}) copy-start(bf16[512,512]{1,0:T(8,128)(2,1)} %param.17) | copy-start | bytes 1572868
  11.7 0.6 copy-start.28
  16.6 16.5 %all-to-all-start.1 = ((s32[32,16,1]{1,2,0:T(1,128)}), s32[32,16,1]{1,2,0:T(1,128)S(1)}, u32[]{:S(2)}, u32[]{:S(2)}) async-start(s32[32,16,1]{1,2,0:T(1,128)} %bitcast.2), calls=%async_computation.1 | async-start | bytes 32768 | tf_op jit(solution)/shard_map/all_to_all | solution.py:147
  28.9 22.8 %copy-start.19 = (bf16[64,512]{1,0:T(8,128)(2,1)S(1)}, bf16[64,512]{1,0:T(8,128)(2,1)}, u32[]{:S(2)}) copy-start(bf16[64,512]{1,0:T(8,128)(2,1)} %param.22) | copy-start | bytes 196612
  28.9 22.8 %copy-start.20 = (bf16[64,512]{1,0:T(8,128)(2,1)S(1)}, bf16[64,512]{1,0:T(8,128)(2,1)}, u32[]{:S(2)}) copy-start(bf16[64,512]{1,0:T(8,128)(2,1)} %param.25) | copy-start | bytes 196612
  28.9 22.8 %copy-start.21 = (bf16[64,64]{1,0:T(8,128)(2,1)S(1)}, bf16[64,64]{1,0:T(8,128)(2,1)}, u32[]{:S(2)}) copy-start(bf16[64,64]{1,0:T(8,128)(2,1)} %param.23) | copy-start | bytes 24580
  28.9 22.8 %copy-start.22 = (bf16[64,64]{1,0:T(8,128)(2,1)S(1)}, bf16[64,64]{1,0:T(8,128)(2,1)}, u32[]{:S(2)}) copy-start(bf16[64,64]{1,0:T(8,128)(2,1)} %param.24) | copy-start | bytes 24580
  28.9 23.7 %copy-start.25 = (s32[512]{0:T(512)S(1)}, s32[512]{0:T(512)}, u32[]{:S(2)}) copy-start(s32[512]{0:T(512)} %param.20) | copy-start | bytes 6148
  33.1 49.0 %copy-start.16 = (s32[32,16,1]{1,2,0:T(1,128)}, s32[32,16,1]{1,2,0:T(1,128)S(1)}, u32[]{:S(2)}) copy-start(s32[32,16,1]{1,2,0:T(1,128)S(1)} %all-to-all-done.1) | copy-start | bytes 6148
  33.1 15.9 %all-to-all-start = ((bf16[32,16,512]{2,1,0:T(8,128)(2,1)}), bf16[32,16,512]{2,1,0:T(8,128)(2,1)S(1)}, u32[]{:S(2)}, u32[]{:S(2)}) async-start(bf16[32,16,512]{2,1,0:T(8,128)(2,1)} %bitcast), calls=%async_computation | async-start | bytes 1048576 | tf_op jit(solution)/shard_map/all_to_all | solution.py:145
  37.3 42.7 %all-gather.11.cloned.1.call-start = ((), (), s32[]{:S(2)}) async-start(), calls=%async_computation.13 | async-start | bytes 2621440 | tf_op jit(solution)/shard_map/all_gather | solution.py:151
  48.9 81.4 %copy-start.23 = (f32[2048]{0:T(1024)S(1)}, f32[2048]{0:T(1024)}, u32[]{:S(2)}) copy-start(f32[2048]{0:T(1024)} %param.21) | copy-start | bytes 24580
  51.6 78.8 %all-gather.7.cloned.1.call-start = ((), (), s32[]{:S(2)}) async-start(), calls=%async_computation.7 | async-start | bytes 4866048 | tf_op jit(solution)/shard_map/all_gather | solution.py:99
  52.5 210.3 %all-reduce.4.cloned.1.call-start = ((), (), s32[]{:S(2)}) async-start(), calls=%async_computation.8 | async-start | bytes 8388608 | tf_op jit(solution)/shard_map/psum | solution.py:194
  53.1 84.4 %copy-start.30 = (f32[32]{0:T(128)}, f32[32]{0:T(128)S(1)}, u32[]{:S(2)}) copy-start(f32[32]{0:T(128)S(1)} %negate_power_fusion) | copy-start | bytes 388
  134.0 1.7 copy-start.5
  135.6 4.5 copy-start.26
  165.2 0.8 copy-start.9
  171.0 1.0 copy-start.4
  171.0 124.6 %all-gather.13.cloned.1.call-start = ((), (), s32[]{:S(2)}) async-start(), calls=%async_computation.14 | async-start | bytes 2621440 | tf_op jit(solution)/shard_map/all_gather | solution.py:152
  190.6 2.7 copy-start.14
  190.6 2.7 copy-start.15
  193.3 179.1 %all-gather.9.cloned.1.call-start = ((), (), s32[]{:S(2)}) async-start(), calls=%async_computation.9 | async-start | bytes 17842176 | tf_op jit(solution)/shard_map/all_gather | solution.py:99
  195.1 72.5 %copy-start.18 = (f32[2048]{0:T(1024)S(1)}, f32[2048]{0:T(1024)}, u32[]{:S(2)}) copy-start(f32[2048]{0:T(1024)} %param.26) | copy-start | bytes 24580
  195.1 300.7 %all-reduce.6.cloned.1.call-start = ((), (), s32[]{:S(2)}) async-start(), calls=%async_computation.11 | async-start | bytes 8388608 | tf_op jit(solution)/shard_map/psum | solution.py:217
  265.6 2.1 copy-start.2
  372.4 6.6 copy-start.11
  372.4 8.9 copy-start.31
  393.6 5.4 copy-start.32
  404.0 230.1 %all-reduce.8.cloned.1.call-start = ((), (), s32[]{:S(2)}) async-start(), calls=%async_computation.12 | async-start | bytes 4194304 | tf_op jit(solution)/shard_map/psum | solution.py:253
  495.9 4.6 copy-start.3
  495.9 5.9 copy-start.6
  504.4 1.9 copy-start.7
  506.4 5.2 copy-start.27
  575.4 187.3 %reduce-scatter.5.cloned.1.call-start = ((), (), s32[]{:S(2)}) async-start(), calls=%async_computation.10 | async-start | bytes 2621440 | tf_op jit(solution)/shard_map/reduce_scatter | solution.py:204
  583.4 310.8 %reduce-scatter.7.cloned.1.call-start = ((), (), s32[]{:S(2)}) async-start(), calls=%async_computation.15 | async-start | bytes 23248896
  583.4 8.0 copy-start.12
  583.5 7.9 copy-start.34
  591.4 5.3 copy-start.13
  591.4 5.3 copy-start.33
  596.7 5.0 copy-start.24
  603.3 2.8 copy-start.8
  603.3 2.7 copy-start.10
  761.9 0.7 copy-start.17
  766.9 19.3 %all-to-all-start.2 = ((bf16[32,16,512]{2,1,0:T(8,128)(2,1)}), bf16[32,16,512]{2,1,0:T(8,128)(2,1)S(1)}, u32[]{:S(2)}, u32[]{:S(2)}) async-start(bf16[32,16,512]{2,1,0:T(8,128)(2,1)} %bitcast.14), calls=%async_computation.3 | async-start | bytes 1048576 | tf_op jit(solution)/shard_map/all_to_all | solution.py:281
  774.6 15.9 %copy-start.29 = (s32[512]{0:T(512)S(1)}, s32[512]{0:T(512)}, u32[]{:S(2)}) copy-start(s32[512]{0:T(512)} %copy-done.28) | copy-start | bytes 6148
  786.1 15.9 %all-to-all-start.4 = ((bf16[32,16,512]{2,1,0:T(8,128)(2,1)}), bf16[32,16,512]{2,1,0:T(8,128)(2,1)S(1)}, u32[]{:S(2)}, u32[]{:S(2)}) async-start(bf16[32,16,512]{2,1,0:T(8,128)(2,1)} %bitcast.24), calls=%async_computation.5 | async-start | bytes 1048576 | tf_op jit(solution)/shard_map/all_to_all | solution.py:282
  897.2 10.4 %copy-start.1 = (bf16[512,512]{1,0:T(8,128)(2,1)S(1)}, bf16[512,512]{1,0:T(8,128)(2,1)}, u32[]{:S(2)}) copy-start(bf16[512,512]{1,0:T(8,128)(2,1)} %param.17) | copy-start | bytes 1572868
Sparse Core Ops, SparseCore 0:
  51.7 28.2 all-gather.10
  82.8 47.4 all-gather.6
  171.1 91.5 all-reduce.3
  264.9 30.6 all-gather.12
  298.0 74.3 all-gather.8
  404.1 91.7 all-reduce.5
  575.6 58.4 all-reduce.7
  636.6 29.4 reduce-scatter.4
  762.0 132.1 reduce-scatter.6
where the time goes:
time: 928 us; the launch traced here: 915 us
  waiting for transfers between devices  465 us (50%)
  local copies, waits for them, and re-layouts  191 us (21%)
  matrix products  142 us (15%)
  other arithmetic  49.6 us (5%)
  starting transfers between devices  36.1 us (4%)
  blocking collectives  16.6 us (2%)
  between operations  14.9 us (2%)
    dot_general x77, matrix products, matmul(): return jnp.dot(left, right, preferred_element_type=jnp.float32)  142 us
    all_gather x2, waiting for transfers between devices, gather_rows(): lax.all_gather(jnp.concatenate(parts, axis=1), 'row', axis=0, tiled=True)  125 us
    concatenate x1, local copies, waits for them, and re-layouts, scatter_rows(): jnp.concatenate(columns, axis=1)  93.2 us
    unnamed x10, waiting for transfers between devices  89.6 us
    psum x1, waiting for transfers between devices, body(): normed_grad_two = lax.psum(normed_terms_two, 'col')  82.1 us
    psum x1, waiting for transfers between devices, body(): attn_full = lax.psum(attn_terms, 'col')  67.6 us
    unnamed x82, local copies, waits for them, and re-layouts  51.5 us
    all_gather x1, waiting for transfers between devices, body(): lax.all_gather(arrived_rows[placing], 'col', axis=1, tiled=True)  26.4 us
  transfers between devices with their start and end apart: 13, of which 12 were waited for; matrix products, arithmetic and copies ran while one was open for 22% of the time, Pallas kernels for 0%

commit v1 on v0

--- a/solution.py
+++ b/solution.py
@@ -191,7 +191,11 @@
         .astype(jnp.bfloat16)
     )
     attn_terms = matmul(mixed, output_w.T)
-    attn_full = lax.psum(attn_terms, "col")
+    attn_full = attn_terms
+    for hop in (1, 2):
+        attn_full = attn_full + lax.ppermute(
+            attn_full, "col", [(dev, dev ^ hop) for dev in range(4)]
+        )
     resid = rows_wide + attn_full
     inv_two = rms_scale(resid)
     normed_two = (resid * inv_two * ffn_gain).astype(jnp.bfloat16)

time: 928 us -> 928 us (level)
  matrix products: 142 us -> 154 us
    ppermute x0 -> x2, waiting for transfers between devices: none -> 181 us  [body(): lax.ppermute(attn_full, 'col', [(dev, dev ^ hop) for dev in range(4)])]
    all_gather x2, waiting for transfers between devices: 125 us -> 48.2 us  [gather_rows(): lax.all_gather(jnp.concatenate(parts, axis=1), 'row', axis=0, tiled=True)]
    psum x1 -> x0, waiting for transfers between devices: 67.6 us -> none  [body(): attn_full = lax.psum(attn_terms, 'col')]
    all_gather x1, waiting for transfers between devices: 26.3 us -> 0.01 us  [body(): lax.all_gather(arrived_grads[placing], 'col', axis=1, tiled=True)]
    all_gather x1, waiting for transfers between devices: 26.4 us -> 5.15 us  [body(): lax.all_gather(arrived_rows[placing], 'col', axis=1, tiled=True)]
    dot_general x77, matrix products: 142 us -> 154 us  [matmul(): return jnp.dot(left, right, preferred_element_type=jnp.float32)]
    psum x1, waiting for transfers between devices: 82.1 us -> 92.9 us  [body(): normed_grad_two = lax.psum(normed_terms_two, 'col')]
    unnamed x82 -> x84, local copies, waits for them, and re-layouts: 51.5 us -> 49 us
  transfers between devices with their start and end apart: 13 -> 14, of which waited for: 12 -> 11; matrix products, arithmetic and copies ran while one was open for 22% -> 26% of each run, Pallas kernels for 0% -> 0%
where the time goes in v1:
time: 928 us; the launch traced here: 917 us
  waiting for transfers between devices  463 us (50%)
  local copies, waits for them, and re-layouts  189 us (20%)
  matrix products  154 us (17%)
  other arithmetic  49.4 us (5%)
  starting transfers between devices  30.9 us (3%)
  blocking collectives  15.4 us (2%)
  between operations  15 us (2%)
    ppermute x2, waiting for transfers between devices, body(): lax.ppermute(attn_full, 'col', [(dev, dev ^ hop) for dev in range(4)])  181 us
    dot_general x77, matrix products, matmul(): return jnp.dot(left, right, preferred_element_type=jnp.float32)  154 us
    concatenate x1, local copies, waits for them, and re-layouts, scatter_rows(): jnp.concatenate(columns, axis=1)  93.5 us
    psum x1, waiting for transfers between devices, body(): normed_grad_two = lax.psum(normed_terms_two, 'col')  92.9 us
    unnamed x9, waiting for transfers between devices  89.5 us
    unnamed x84, local copies, waits for them, and re-layouts  49 us
    all_gather x2, waiting for transfers between devices, gather_rows(): lax.all_gather(jnp.concatenate(parts, axis=1), 'row', axis=0, tiled=True)  48.2 us
    psum x1, waiting for transfers between devices, body(): lax.psum(normed_terms_one.astype(jnp.bfloat16), 'col').astype(jnp.float32)  24.7 us
  transfers between devices with their start and end apart: 14, of which 11 were waited for; matrix products, arithmetic and copies ran while one was open for 26% of the time, Pallas kernels for 0%

profile of v1, /device:TPU:1, one launch (start us, length us, event | category | flops | bytes accessed | tf_op | source)
XLA Modules:
  0.0 917.1 jit_solution(2304889747308429456)
XLA Ops:
  7.2 4.5 sort.45
  12.3 3.6 gather_fusion.1
  16.6 9.6 %all-to-all-start.1 = ((s32[32,16,1]{1,2,0:T(1,128)}), s32[32,16,1]{1,2,0:T(1,128)S(1)}, u32[]{:S(2)}, u32[]{:S(2)}) async-start(s32[32,16,1]{1,2,0:T(1,128)} %bitcast.2), calls=%async_computation.1 | async-start | bytes 32768 | tf_op jit(solution)/shard_map/all_to_all | solution.py:147
  26.2 2.6 gather_fusion
  28.9 4.2 all-to-all-done.1
  33.1 4.2 all-to-all-start
  38.6 3.8 sort.46
  42.4 6.5 all-to-all-done
  48.9 2.6 gather_fusion.2
  52.5 2.0 gather_fusion.5
  54.6 15.4 %all_to_all.60 = bf16[32,16,512]{2,1,0:T(8,128)(2,1)S(1)} all-to-all(bf16[32,16,512]{2,1,0:T(8,128)(2,1)S(1)} %bitcast.184), channel_id=1, replica_groups=mesh['row'=32,'col'=4] {'row'}, dimensions={0} | all-to-all | bytes 1048576 | tf_op jit(solution)/shard_map/all_to_all | solution.py:146
  69.9 2.6 gather_fusion.6
  74.9 5.1 all-gather.11.cloned.1.call-done
  80.0 2.1 fusion.54
  82.1 48.2 %all-gather.7.cloned.1.call-done = bf16[2048,1152]{1,0:T(8,128)(2,1)} async-done(((bf16[64,1152]{1,0:T(8,128)(2,1)}), bf16[2048,1152]{1,0:T(8,128)(2,1)}) %all-gather.7.cloned.1.call-update) | async-done | bytes 4718608 | tf_op jit(solution)/shard_map/all_gather | solution.py:99
  130.3 3.6 fusion.67
  135.6 1.9 convolution_bitcast_fusion.2
  138.0 2.0 fusion.72
  140.2 25.1 %while.32 = (s32[]{:T(128)}, bf16[8,512,64]{1,2,0:T(8,128)(2,1)S(1)}, f32[8,512]{1,0:T(8,128)}, bf16[8,512,64]{2,1,0:T(8,128)(2,1)}, bf16[1,512,64]{2,1,0:T(8,12...) while((s32[]{:T(128)}, bf16[8,512,64]{1,2,0:T(8,128)(2,1)S(1)}, ...), condition=%wide.region_8.9_spmd.clone.clone, body=%wide.region_5.8_spmd.clone.sunk.clone | while | flops 69991936 | bytes 3694689 | solution.py:178
  165.3 2.9 fusion.63
  169.4 90.8 %collective-permute-done = f32[512,2048]{1,0:T(8,128)S(1)} collective-permute-done((f32[512,2048]{1,0:T(8,128)S(1)}, f32[512,2048]{1,0:T(8,128)S(1)}, u32[]{:S(2)}, u32[]{:S(2)}) %collective-permute-start) | collective-permute-done | bytes 4194336 | tf_op jit(solution)/shard_map/ppermute | solution.py:196
  261.0 3.0 collective-permute-start.1
  263.9 89.9 %collective-permute-done.1 = f32[512,2048]{1,0:T(8,128)S(1)} collective-permute-done((f32[512,2048]{1,0:T(8,128)S(1)}, f32[512,2048]{1,0:T(8,128)S(1)}, u32[]{:S(2)}, u32[]{:S(2)}) %collective-permute-start.1) | collective-permute-done | bytes 4194336 | tf_op jit(solution)/shard_map/ppermute | solution.py:196
  355.0 2.1 copy-done.2
  358.7 6.6 fusion.41
  365.3 2.3 copy-done.32
  367.6 5.0 fusion.47
  372.6 7.3 multiply_convert_fusion.4
  380.0 5.4 fusion.45
  385.3 5.1 fusion.55
  390.9 92.9 %all-reduce.3.cloned.1.call-done = f32[512,2048]{1,0:T(8,128)} async-done(((f32[512,2048]{1,0:T(8,128)}), f32[512,2048]{1,0:T(8,128)}) %all-reduce.3.cloned.1.call-update) | async-done | bytes 4194320 | tf_op jit(solution)/shard_map/psum | solution.py:221
  483.9 4.6 multiply_reduce_fusion.1
  489.8 2.7 multiply_add_fusion
  492.5 1.9 copy-done.7
  494.4 2.9 fusion.69
  498.7 65.3 %while.33 = (s32[]{:T(128)}, f32[8,512,64]{1,2,0:T(8,128)}, f32[8,512,64]{1,2,0:T(8,128)}, f32[8,512,64]{1,2,0:T(8,128)}, bf16[8,512,64]{2,1,0:T(8,128)(2,1)}, /...) while((s32[]{:T(128)}, f32[8,512,64]{1,2,0:T(8,128)}, ...), condition=%wide.region_16.17_spmd.clone.clone, body=%wide.region_14.16_spmd.clone.sunk.clone | while | flops 170982912 | bytes 9060477 | solution.py:228
  545.8 1.9 fusion.177
  552.1 1.9 fusion.176
  564.0 2.1 add_convert_fusion.2
  570.7 2.9 fusion.65
  575.4 3.2 add_convert_fusion
  578.6 7.9 fusion.58
  586.6 7.9 convolution_convert_fusion.2
  594.6 5.2 convolution_convert_fusion.1
  599.8 5.1 convolution_convert_fusion
  607.2 2.8 convolution_convert_fusion.4
  609.9 2.6 convolution_convert_fusion.3
  612.6 24.7 %all-reduce.5.cloned.1.call-done = bf16[512,2048]{1,0:T(8,128)(2,1)} async-done(((bf16[512,2048]{1,0:T(8,128)(2,1)}), bf16[512,2048]{1,0:T(8,128)(2,1)}) %all-reduce.5.cloned.1.call-update) | async-done | bytes 2097168 | tf_op jit(solution)/shard_map/psum | solution.py:257
  637.3 6.2 fusion.53
  643.5 93.5 %concatenate.53 = bf16[2048,5378]{0,1:T(8,128)(2,1)} concatenate(bf16[2048,512]{0,1:T(8,128)(2,1)} %convolution_convert_fusion.4, bf16[2048,64]{0,1:T(8,128)(2,1)S(1)} %convolution_convert_fusion.6, bf16[2048,64]{0,1:T(8,128)(2,1)S(1)} %copy-done.12, bf16[2048,512]{0,1:T(8,128)(2,1)} %convolution_convert_fusion.3, bf16[2048,1408]{0,1:T(8,128)(2,1)} %convolution_convert_fusion.2, ...), dimensions={1} | concatenate | bytes 44056576 | tf_op jit(solution)/shard_map/concatenate | solution.py:112
  737.0 27.4 %copy.67 = bf16[2048,5378]{1,0:T(8,128)(2,1)} copy(bf16[2048,5378]{0,1:T(8,128)(2,1)} %concatenate.53) | data formatting | bytes 44056576
  766.8 2.6 gather_fusion.3
  769.4 7.7 all-to-all-start.2
  777.2 2.5 fusion.73
  779.7 2.6 gather_fusion.7
  782.3 6.4 all-to-all-done.2
  788.7 4.3 all-to-all-start.4
  793.0 3.8 sort.47
  796.8 2.6 gather_fusion.4
  799.4 5.1 all-to-all-done.4
  804.6 2.6 gather_fusion.8
  807.2 89.4 %reduce-scatter.7.cloned.1.call-done = bf16[64,5378]{1,0:T(8,128)(2,1)} async-done(((bf16[2048,5378]{1,0:T(8,128)(2,1)}), bf16[64,5378]{1,0:T(8,128)(2,1)}) %reduce-scatter.7.cloned.1.call-update) | async-done | bytes 688400
  896.6 2.0 copy.68
  906.0 2.1 copy.64
  (252 shorter events, 123.1 us)
Async XLA Ops:
  7.2 19.0 %copy-start = (bf16[512,512]{1,0:T(8,128)(2,1)S(1)}, bf16[512,512]{1,0:T(8,128)(2,1)}, u32[]{:S(2)}) copy-start(bf16[512,512]{1,0:T(8,128)(2,1)} %param.17) | copy-start | bytes 1572868
  11.7 0.6 copy-start.28
  16.6 16.5 %all-to-all-start.1 = ((s32[32,16,1]{1,2,0:T(1,128)}), s32[32,16,1]{1,2,0:T(1,128)S(1)}, u32[]{:S(2)}, u32[]{:S(2)}) async-start(s32[32,16,1]{1,2,0:T(1,128)} %bitcast.2), calls=%async_computation.1 | async-start | bytes 32768 | tf_op jit(solution)/shard_map/all_to_all | solution.py:147
  28.9 22.8 %copy-start.19 = (bf16[64,512]{1,0:T(8,128)(2,1)S(1)}, bf16[64,512]{1,0:T(8,128)(2,1)}, u32[]{:S(2)}) copy-start(bf16[64,512]{1,0:T(8,128)(2,1)} %param.22) | copy-start | bytes 196612
  28.9 22.8 %copy-start.20 = (bf16[64,512]{1,0:T(8,128)(2,1)S(1)}, bf16[64,512]{1,0:T(8,128)(2,1)}, u32[]{:S(2)}) copy-start(bf16[64,512]{1,0:T(8,128)(2,1)} %param.25) | copy-start | bytes 196612
  28.9 22.8 %copy-start.21 = (bf16[64,64]{1,0:T(8,128)(2,1)S(1)}, bf16[64,64]{1,0:T(8,128)(2,1)}, u32[]{:S(2)}) copy-start(bf16[64,64]{1,0:T(8,128)(2,1)} %param.23) | copy-start | bytes 24580
  28.9 22.8 %copy-start.22 = (bf16[64,64]{1,0:T(8,128)(2,1)S(1)}, bf16[64,64]{1,0:T(8,128)(2,1)}, u32[]{:S(2)}) copy-start(bf16[64,64]{1,0:T(8,128)(2,1)} %param.24) | copy-start | bytes 24580
  28.9 23.7 %copy-start.4 = (bf16[512,512]{1,0:T(8,128)(2,1)S(1)}, bf16[512,512]{1,0:T(8,128)(2,1)}, u32[]{:S(2)}) copy-start(bf16[512,512]{1,0:T(8,128)(2,1)} %param.18) | copy-start | bytes 1572868
  33.1 19.4 %copy-start.16 = (s32[32,16,1]{1,2,0:T(1,128)}, s32[32,16,1]{1,2,0:T(1,128)S(1)}, u32[]{:S(2)}) copy-start(s32[32,16,1]{1,2,0:T(1,128)S(1)} %all-to-all-done.1) | copy-start | bytes 6148
  33.1 15.9 %all-to-all-start = ((bf16[32,16,512]{2,1,0:T(8,128)(2,1)}), bf16[32,16,512]{2,1,0:T(8,128)(2,1)S(1)}, u32[]{:S(2)}, u32[]{:S(2)}) async-start(bf16[32,16,512]{2,1,0:T(8,128)(2,1)} %bitcast), calls=%async_computation | async-start | bytes 1048576 | tf_op jit(solution)/shard_map/all_to_all | solution.py:145
  37.3 42.7 %all-gather.11.cloned.1.call-start = ((), (), s32[]{:S(2)}) async-start(), calls=%async_computation.12 | async-start | bytes 2621440 | tf_op jit(solution)/shard_map/all_gather | solution.py:151
  51.6 78.8 %all-gather.7.cloned.1.call-start = ((), (), s32[]{:S(2)}) async-start(), calls=%async_computation.7 | async-start | bytes 4866048 | tf_op jit(solution)/shard_map/all_gather | solution.py:99
  52.5 306.3 %all-gather.13.cloned.1.call-start = ((), (), s32[]{:S(2)}) async-start(), calls=%async_computation.13 | async-start | bytes 2621440 | tf_op jit(solution)/shard_map/all_gather | solution.py:152
  54.5 18.1 %copy-start.13 = (bf16[64,1408]{1,0:T(8,128)(2,1)S(1)}, bf16[64,1408]{1,0:T(8,128)(2,1)}, u32[]{:S(2)}) copy-start(bf16[64,1408]{1,0:T(8,128)(2,1)} %param.29) | copy-start | bytes 540676
  54.5 18.1 %copy-start.14 = (bf16[64,1408]{1,0:T(8,128)(2,1)S(1)}, bf16[64,1408]{1,0:T(8,128)(2,1)}, u32[]{:S(2)}) copy-start(bf16[64,1408]{1,0:T(8,128)(2,1)} %param.28) | copy-start | bytes 540676
  54.5 18.1 %copy-start.15 = (bf16[64,1408]{1,0:T(8,128)(2,1)S(1)}, bf16[64,1408]{1,0:T(8,128)(2,1)}, u32[]{:S(2)}) copy-start(bf16[64,1408]{1,0:T(8,128)(2,1)} %param.27) | copy-start | bytes 540676
  54.5 19.2 %copy-start.26 = (s32[512]{0:T(512)S(1)}, s32[512]{0:T(512)}, u32[]{:S(2)}) copy-start(s32[512]{0:T(512)} %param.20) | copy-start | bytes 6148
  69.9 60.4 %copy-start.23 = (f32[2048]{0:T(1024)S(1)}, f32[2048]{0:T(1024)}, u32[]{:S(2)}) copy-start(f32[2048]{0:T(1024)} %param.21) | copy-start | bytes 24580
  72.5 286.2 %all-gather.9.cloned.1.call-start = ((), (), s32[]{:S(2)}) async-start(), calls=%async_computation.8 | async-start | bytes 17842176 | tf_op jit(solution)/shard_map/all_gather | solution.py:99
  73.5 410.4 %all-reduce.3.cloned.1.call-start = ((), (), s32[]{:S(2)}) async-start(), calls=%async_computation.10 | async-start | bytes 8388608 | tf_op jit(solution)/shard_map/psum | solution.py:221
  74.3 0.6 copy-start.30
  134.0 1.7 copy-start.5
  134.0 3.5 copy-start.31
  168.2 92.0 %collective-permute-start = (f32[512,2048]{1,0:T(8,128)S(1)}, f32[512,2048]{1,0:T(8,128)S(1)}, u32[]{:S(2)}, u32[]{:S(2)}) collective-permute-start(f32[512,2048]{1,0:T(8,128)S(1)} %fusion.63), channel_id=1, source_target_pairs={{0,1},{1,0},{2,3},{3,2},{4,5},{5,4},{6,7},{7,6},{8,9},{9,8},{10,11... | collective-permute-start | bytes 12582920 | tf_op jit(solution)/shard_map/ppermute | solution.py:196
  261.0 96.1 %copy-start.18 = (f32[2048]{0:T(1024)S(1)}, f32[2048]{0:T(1024)}, u32[]{:S(2)}) copy-start(f32[2048]{0:T(1024)} %param.26) | copy-start | bytes 24580
  261.0 92.8 %collective-permute-start.1 = (f32[512,2048]{1,0:T(8,128)S(1)}, f32[512,2048]{1,0:T(8,128)S(1)}, u32[]{:S(2)}, u32[]{:S(2)}) collective-permute-start(f32[512,2048]{1,0:T(8,128)S(1)} %add.146), channel_id=1, source_target_pairs={{0,2},{1,3},{2,0},{3,1},{4,6},{5,7},{6,4},{7,5},{8,10},{9,11},{10,... | collective-permute-start | bytes 12582920 | tf_op jit(solution)/shard_map/ppermute | solution.py:196
  354.9 2.1 copy-start.2
  358.7 6.6 copy-start.9
  358.7 8.9 copy-start.32
  380.0 5.4 copy-start.33
  390.5 246.8 %all-reduce.5.cloned.1.call-start = ((), (), s32[]{:S(2)}) async-start(), calls=%async_computation.11 | async-start | bytes 4194304 | tf_op jit(solution)/shard_map/psum | solution.py:257
  483.9 4.6 copy-start.3
  483.9 5.9 copy-start.6
  492.5 1.9 copy-start.7
  494.4 4.3 copy-start.27
  578.6 186.7 %reduce-scatter.5.cloned.1.call-start = ((), (), s32[]{:S(2)}) async-start(), calls=%async_computation.9 | async-start | bytes 2621440 | tf_op jit(solution)/shard_map/reduce_scatter | solution.py:208
  586.6 310.0 %reduce-scatter.7.cloned.1.call-start = ((), (), s32[]{:S(2)}) async-start(), calls=%async_computation.14 | async-start | bytes 23248896
  586.6 7.9 copy-start.10
  586.6 7.9 copy-start.35
  594.6 5.2 copy-start.11
  594.6 5.2 copy-start.34
  599.8 5.1 copy-start.24
  607.2 2.8 copy-start.8
  609.9 27.4 %copy-start.25 = (f32[2048]{0:T(1024)S(1)}, f32[2048]{0:T(1024)}, u32[]{:S(2)}) copy-start(f32[2048]{0:T(1024)} %param.21) | copy-start | bytes 24580
  612.6 30.9 %copy-start.12 = (bf16[2048,64]{0,1:T(8,128)(2,1)S(1)}, bf16[2048,64]{0,1:T(8,128)(2,1)}, u32[]{:S(2)}) copy-start(bf16[2048,64]{0,1:T(8,128)(2,1)} %convolution_convert_fusion.5) | copy-start | bytes 786436
  764.4 0.7 copy-start.17
  769.4 19.2 %all-to-all-start.2 = ((bf16[32,16,512]{2,1,0:T(8,128)(2,1)}), bf16[32,16,512]{2,1,0:T(8,128)(2,1)S(1)}, u32[]{:S(2)}, u32[]{:S(2)}) async-start(bf16[32,16,512]{2,1,0:T(8,128)(2,1)} %bitcast.14), calls=%async_computation.3 | async-start | bytes 1048576 | tf_op jit(solution)/shard_map/all_to_all | solution.py:285
  777.1 15.9 %copy-start.29 = (s32[512]{0:T(512)S(1)}, s32[512]{0:T(512)}, u32[]{:S(2)}) copy-start(s32[512]{0:T(512)} %copy-done.28) | copy-start | bytes 6148
  788.7 15.9 %all-to-all-start.4 = ((bf16[32,16,512]{2,1,0:T(8,128)(2,1)}), bf16[32,16,512]{2,1,0:T(8,128)(2,1)S(1)}, u32[]{:S(2)}, u32[]{:S(2)}) async-start(bf16[32,16,512]{2,1,0:T(8,128)(2,1)} %bitcast.24), calls=%async_computation.5 | async-start | bytes 1048576 | tf_op jit(solution)/shard_map/all_to_all | solution.py:286
  899.6 10.5 %copy-start.1 = (bf16[512,512]{1,0:T(8,128)(2,1)S(1)}, bf16[512,512]{1,0:T(8,128)(2,1)}, u32[]{:S(2)}) copy-start(bf16[512,512]{1,0:T(8,128)(2,1)} %param.17) | copy-start | bytes 1572868
Sparse Core Ops, SparseCore 0:
  51.7 28.2 all-gather.10
  82.8 47.4 all-gather.6
  132.6 29.6 all-gather.12
  164.4 74.3 all-gather.8
  390.6 93.2 all-reduce.2
  578.7 58.5 all-reduce.4
  639.7 29.5 reduce-scatter.4
  764.6 131.9 reduce-scatter.6
